TPU v7x, 32 devices: a whole 2x2x4 slice. The times are simulated.
32 devices in a mesh: tile: 8 (over y, x, core), body: 4 (over z).
Axes of the slice: x: 2, y: 2, z: 4, core: 2. Of those that a mesh axis runs over, the one named last changes fastest.
Arguments:
- fluid_position: float32 [3, 128, 32, 128], P(None, 'tile', 'body'), may hold values from 0 to 128, as said below
- fluid_pressure: float32 [128, 32, 128], P('tile', 'body'), may hold values from 0 to 1
- source: float32 [128, 32, 128], P('tile', 'body'), may hold values from -12 to 12
- stiffness: float32 [128, 32, 128], P('tile', 'body'), may hold values from 0.5 to 2
- neighbours: int32 [128, 32, 6], P('tile', 'body'), may hold values from 0 to 8, as said below
- wall_position: float32 [3, 128, 32, 128], P(None, 'tile', 'body'), may hold values from 0 to 128, as said below
- wall_normal: float32 [3, 128, 32, 128], P(None, 'tile', 'body'), may hold values from -4 to 4
- wall_arm: float32 [3, 128, 32, 128], P(None, 'tile', 'body'), may hold values from -4 to 4
- wall_live: int32 [128, 32, 128], P('tile', 'body'), may hold values 0 or 1
- wall_body: int32 [128, 32, 128], P('tile', 'body'), may hold values from 0 to 30719, as said below
- linear_velocity: float32 [3, 30720], P(None, 'body'), may hold values from -6 to 6
- angular_velocity: float32 [3, 30720], P(None, 'body'), may hold values from -6 to 6
- inverse_mass: float32 [30720], P('body'), may hold values from 0.2 to 2
- inverse_inertia: float32 [3, 30720], P(None, 'body'), may hold values from 0.2 to 2
Outputs:
- pressure: float32 [128, 32, 128], P('tile', 'body')
- wall_pressure: float32 [128, 32, 128], P('tile', 'body')
- body_state: float32 [6, 30720], P(None, 'body')
- wall_velocity: float32 [3, 128, 32, 128], P(None, 'tile', 'body')
- density_error: float32 [], replicated
Inputs may be any that keep to these rules, and one draw needn't show every extreme that they name: `neighbours`: entry 0 of every list is 4, the block itself; the other entries are distinct codes of the eight blocks around it. `fluid_position`: A particle of block (a, b) has its first coordinate in [a, a + 1), its second in [b, b + 1), its third in [0, 1). `wall_position`: A particle of block (a, b) has its first coordinate in [a, a + 1], its second in [b, b + 1], its third in [0, 1]. `wall_body`: bodies are compact: a boundary particle belongs to a body whose centre lies within a few blocks of its own block.
All inputs are finite; a program needn't handle non-finite values. No bound on the sum of `wall_live` on one device may be relied on, other than what follows from the above.
Results may differ from a plain program's by a relative error of at most 0.0003.
Values sent between devices are 32-bit elements; how exact they have to be, the bound alone decides.
A program may use at most 128 MiB of HBM per device.

v0:
```python
import jax
import jax.numpy as jnp
from jax import lax
from jax.sharding import PartitionSpec as P

SWEEPS = 2
BODIES = 30720
relax_factor = 0.5
inv_width = 2.0
kernel_scale = 0.0078125
wall_offset = 0.5
time_step = 0.25
gravity_z = -9.81


def padded(block, sides, width):
    for axis, dim in sides:
        count = lax.axis_size(axis)
        forward = [(i, i + 1) for i in range(count - 1)]
        backward = [(target, source) for source, target in forward]
        low = lax.ppermute(
            lax.slice_in_dim(block, block.shape[dim] - width, None, axis=dim), axis, forward
        )
        high = lax.ppermute(lax.slice_in_dim(block, 0, width, axis=dim), axis, backward)
        block = jnp.concatenate([low, block, high], axis=dim)
    return block


def pair_sums(padded_pos, padded_val, own_pos, neighbours):
    row_count = own_pos.shape[1]
    columns = own_pos.shape[2]

    def one_row(row_index):
        window_pos = lax.dynamic_slice_in_dim(padded_pos, row_index, 3, 1)
        window_val = lax.dynamic_slice_in_dim(padded_val, row_index, 3, 0)
        shifted_pos = jnp.stack(
            [window_pos[:, i, j : j + columns] for i in range(3) for j in range(3)], 0
        )
        shifted_val = jnp.stack(
            [window_val[i, j : j + columns] for i in range(3) for j in range(3)], 0
        )
        code_list = lax.dynamic_index_in_dim(neighbours, row_index, 0, keepdims=False)
        near_pos = jnp.take_along_axis(
            jnp.transpose(shifted_pos, (2, 0, 1, 3)), code_list[:, :, None, None], axis=1
        )
        near_val = jnp.take_along_axis(
            jnp.transpose(shifted_val, (1, 0, 2)), code_list[:, :, None], axis=1
        )
        own_rows = lax.dynamic_index_in_dim(own_pos, row_index, 1, keepdims=False)
        distance = None
        for component in range(3):
            offset = (
                own_rows[component][:, None, :, None] - near_pos[:, :, component][:, :, None, :]
            )
            distance = offset * offset if distance is None else distance + offset * offset
        weight = jnp.exp(-distance * inv_width) * kernel_scale
        weight_sum = jnp.sum(weight, axis=(1, 3))
        weighted = jnp.einsum("ckij,ckj->ci", weight, near_val, precision=lax.Precision.HIGHEST)
        return (weight_sum, weighted)

    return lax.map(one_row, jnp.arange(row_count, dtype=jnp.int32))


def cross_product(left, right):
    return jnp.stack(
        [
            left[1] * right[2] - left[2] * right[1],
            left[2] * right[0] - left[0] * right[2],
            left[0] * right[1] - left[1] * right[0],
        ],
        0,
    )


def advance(params, totals):
    lift = jnp.array([0.0, 0.0, time_step * gravity_z], dtype=jnp.float32)[:, None]
    linear = params[0:3] + time_step * (params[6][None] * totals[0:3]) + lift
    angular = params[3:6] + time_step * params[7:10] * totals[3:6]
    return jnp.concatenate([linear, angular], 0)


def widened(values):
    return padded(values, (("tile", 0), ("body", 1)), 1)


def shards(
    fluid_position,
    fluid_pressure,
    source,
    stiffness,
    neighbours,
    wall_position,
    wall_normal,
    wall_arm,
    wall_live,
    wall_body,
    linear_velocity,
    angular_velocity,
    inverse_mass,
    inverse_inertia,
):
    padded_pos = padded(fluid_position, (("tile", 1), ("body", 2)), 1)
    pressure = fluid_pressure
    residual = source
    for sweep_index in range(SWEEPS):
        weight_sum, weighted = pair_sums(padded_pos, widened(pressure), fluid_position, neighbours)
        diagonal = stiffness + weight_sum
        residual = source - (diagonal * pressure - weighted)
        pressure = jnp.maximum(pressure + relax_factor * residual / diagonal, 0.0)
    particle_total = residual.size * lax.axis_size("tile") * lax.axis_size("body")
    error_local = jnp.sum(residual * residual) / particle_total
    weight_sum, weighted = pair_sums(padded_pos, widened(pressure), wall_position, neighbours)
    wall_pressure = weighted / (wall_offset + weight_sum) * wall_live.astype(jnp.float32)
    force = wall_pressure[None] * wall_normal
    torque = cross_product(wall_arm, force)
    stacked = jnp.concatenate([force, torque], 0).reshape(6, -1).T
    partials = jax.ops.segment_sum(stacked, wall_body.reshape(-1), num_segments=BODIES).T
    owned = BODIES // lax.axis_size("body")
    first_owned = lax.axis_index("body") * owned
    own_params = jnp.concatenate(
        [linear_velocity, angular_velocity, inverse_mass[None], inverse_inertia], 0
    )
    totals, density_error = lax.psum((partials, error_local), ("tile", "body"))
    all_params = lax.all_gather(own_params, "body", axis=1, tiled=True)
    full_state = advance(all_params, totals)
    own_state = lax.dynamic_slice_in_dim(full_state, first_owned, owned, 1)
    index_flat = wall_body.reshape(-1)
    moving = jnp.take(full_state[0:3], index_flat, axis=1).reshape(wall_arm.shape)
    turning = jnp.take(full_state[3:6], index_flat, axis=1).reshape(wall_arm.shape)
    wall_velocity = moving + cross_product(turning, wall_arm)
    return (pressure, wall_pressure, own_state, wall_velocity, density_error)


def solution(mesh):
    placed = (
        P(None, "tile", "body", None),
        P("tile", "body", None),
        P("tile", "body", None),
        P("tile", "body", None),
        P("tile", "body", None),
        P(None, "tile", "body", None),
        P(None, "tile", "body", None),
        P(None, "tile", "body", None),
        P("tile", "body", None),
        P("tile", "body", None),
        P(None, "body"),
        P(None, "body"),
        P("body"),
        P(None, "body"),
    )
    return jax.shard_map(
        shards,
        mesh=mesh,
        in_specs=placed,
        out_specs=(
            P("tile", "body", None),
            P("tile", "body", None),
            P(None, "body"),
            P(None, "tile", "body", None),
            P(),
        ),
        check_vma=False,
    )
```

profile of v0, /device:TPU:0, one launch (start us, length us, event | category | flops | bytes accessed | tf_op | source)
XLA Modules:
  0.0 1128.1 jit_solution(10268399384290714096)
XLA Ops:
  13.8 4.5 collective-permute-start
  27.3 4.5 collective-permute-start.2
  33.4 4.2 collective-permute-done.3
  37.9 214.2 %while.36 = (s32[]{:T(128)}, f32[16,8,128]{2,1,0:T(8,128)S(1)}, f32[16,8,128]{2,1,0:T(8,128)S(1)}, s32[16]{0:T(128)S(1)}, f32[3,16,8,128]{3,2,1,0:T(8,128)}, /*i...) while((s32[]{:T(128)}, f32[16,8,128]{2,1,0:T(8,128)S(1)}, ...), condition=%wide.region_2.0_spmd, body=%wide.region_0.4_spmd.sunk | while | flops 27549932 | bytes 1204188 | solution.py:61
  60.6 4.0 fusion.81
  74.0 4.0 fusion.81
  87.4 4.0 fusion.81
  100.8 4.0 fusion.81
  114.1 4.0 fusion.81
  127.5 4.0 fusion.81
  140.9 4.0 fusion.81
  154.3 4.0 fusion.81
  167.7 4.0 fusion.81
  181.1 4.0 fusion.81
  194.5 4.0 fusion.81
  207.8 4.0 fusion.81
  254.7 5.0 collective-permute-done.9
  264.7 4.0 collective-permute-done.11
  268.9 214.2 %while.37 = (s32[]{:T(128)}, f32[16,8,128]{2,1,0:T(8,128)S(1)}, f32[16,8,128]{2,1,0:T(8,128)S(1)}, s32[16]{0:T(128)S(1)}, f32[3,16,8,128]{3,2,1,0:T(8,128)}, /*i...) while((s32[]{:T(128)}, f32[16,8,128]{2,1,0:T(8,128)S(1)}, ...), condition=%wide.region_5.8_spmd, body=%wide.region_3.7_spmd.sunk | while | flops 27549932 | bytes 1204188 | solution.py:61
  278.2 4.0 fusion.85
  291.6 4.0 fusion.85
  305.0 4.0 fusion.85
  318.4 4.0 fusion.85
  331.8 4.0 fusion.85
  345.1 4.0 fusion.85
  358.5 4.0 fusion.85
  371.9 4.0 fusion.85
  385.3 4.0 fusion.85
  398.7 4.0 fusion.85
  412.1 4.0 fusion.85
  425.5 4.0 fusion.85
  438.8 4.0 fusion.85
  452.2 4.0 fusion.85
  465.6 4.0 fusion.85
  479.0 4.0 fusion.85
  500.0 214.1 %while.38 = (s32[]{:T(128)}, f32[16,8,128]{2,1,0:T(8,128)S(1)}, f32[16,8,128]{2,1,0:T(8,128)S(1)}, s32[16]{0:T(128)S(1)}, f32[3,16,8,128]{3,2,1,0:T(8,128)}, /*i...) while((s32[]{:T(128)}, f32[16,8,128]{2,1,0:T(8,128)S(1)}, ...), condition=%wide.region_8.11_spmd, body=%wide.region_6.10_spmd.sunk | while | flops 27549932 | bytes 1204188 | solution.py:61
  714.7 5.3 copy.268
  719.9 94.0 %scatter_custom_fusion = f32[30720,6]{1,0:T(8,128)} fusion(s32[16384]{0:T(1024)S(1)} %bitcast.478, f32[16384,6]{1,0:T(8,128)} %copy.268, f32[]{:T(128)} %constant.113.clone.1), kind=kCustom, calls=%fused_computation.226 | custom fusion | flops 98304 | bytes 737792 | tf_op jit(solution)/shard_map/scatter-add | solution.py:117
  814.0 9.5 copy.269
  824.2 41.4 %psum.15 = f32[]{:T(128)} all-reduce(f32[]{:T(128)S(6)} %div.15), channel_id=1, replica_groups=mesh['tile'=8,'body'=4] {'tile','body'}, use_global_device_ids=true, to_apply=%region_12.16 | all-reduce | flops 1 | bytes 8 | tf_op jit(solution)/shard_map/psum | solution.py:123
  866.9 86.6 %all-reduce.2.cloned.1.call-done = f32[6,30720]{1,0:T(8,128)} async-done(((f32[6,30720]{1,0:T(8,128)}), f32[6,30720]{1,0:T(8,128)}) %all-reduce.2.cloned.1.call-update) | async-done | bytes 737296 | tf_op jit(solution)/shard_map/psum | solution.py:123
  956.9 7.7 copy.271
  964.6 7.7 copy.270
  973.2 59.8 %gather_fusion.7 = f32[16384,3]{1,0:T(8,128)} fusion(f32[3,30720]{0,1:T(8,128)} %copy.271, s32[16384]{0:T(1024)S(1)} %fusion.58), kind=kCustom, calls=%fused_computation.7.clone | custom fusion | bytes 458752 | tf_op jit(solution)/shard_map/jit(_take)/gather | solution.py:129
  1033.0 59.9 %gather_fusion.6 = f32[16384,3]{1,0:T(8,128)} fusion(f32[3,30720]{0,1:T(8,128)} %copy.270, s32[16384]{0:T(1024)S(1)} %fusion.58), kind=kCustom, calls=%fused_computation.2.clone | custom fusion | bytes 458752 | tf_op jit(solution)/shard_map/jit(_take)/gather | solution.py:128
  1092.8 10.8 select_bitcast_fusion.3
  1103.6 11.0 slice_reduce_fusion.1
  1114.6 5.2 copy.272
  (1903 shorter events, 414.9 us)
Async XLA Ops:
  8.0 857.6 %all-gather.2.cloned.1.call-start = ((), (), s32[]{:S(2)}) async-start(), calls=%async_computation | async-start | bytes 2457600 | tf_op jit(solution)/shard_map/all_gather | solution.py:124
  8.8 12.5 %collective-permute-start.5 = (f32[1,8,128]{2,1,0:T(8,128)S(1)}, f32[1,8,128]{2,1,0:T(8,128)S(1)}, u32[]{:S(2)}, u32[]{:S(2)}) collective-permute-start(f32[1,8,128]{2,1,0:T(8,128)S(1)} %get-tuple-element.378), channel_id=1, source_target_pairs={{4,0},{8,4},{12,8},{16,12},{20,16},{24,20},{28,24},{5,1},{9,5},{13... | collective-permute-start | bytes 12296 | tf_op jit(solution)/shard_map/ppermute | solution.py:24
  10.0 10.4 collective-permute-start.4
  13.8 12.3 %collective-permute-start = (f32[3,1,8,128]{3,0,2,1:T(4,128)S(1)}, f32[3,1,8,128]{3,0,2,1:T(4,128)S(1)}, u32[]{:S(2)}, u32[]{:S(2)}) collective-permute-start(f32[3,1,8,128]{3,0,2,1:T(4,128)S(1)} %copy.294), channel_id=1, source_target_pairs={{0,4},{4,8},{8,12},{12,16},{16,20},{20,24},{24,28},{1,5},{5,9},{9,... | collective-permute-start | bytes 36872 | tf_op jit(solution)/shard_map/ppermute | solution.py:21
  18.3 8.9 collective-permute-start.1
  21.3 11.8 %collective-permute-start.6 = (f32[18,1,128]{2,1,0:T(1,128)S(1)}, f32[18,1,128]{2,1,0:T(1,128)S(1)}, u32[]{:S(2)}, u32[]{:S(2)}) collective-permute-start(f32[18,1,128]{2,1,0:T(1,128)S(1)} %get-tuple-element.372), channel_id=1, source_target_pairs={{0,1},{1,2},{2,3},{4,5},{5,6},{6,7},{8,9},{9,10},{10,11},{12,13},{... | collective-permute-start | bytes 27656 | tf_op jit(solution)/shard_map/ppermute | solution.py:21
  24.8 8.3 collective-permute-start.7
  27.3 6.2 collective-permute-start.2
  31.8 5.9 collective-permute-start.3
  37.8 214.2 %copy-start.4 = (f32[16,8,128]{2,1,0:T(8,128)S(1)}, f32[16,8,128]{2,1,0:T(8,128)}, u32[]{:S(2)}) copy-start(f32[16,8,128]{2,1,0:T(8,128)} %param.28) | copy-start | bytes 196612
  37.8 214.2 %copy-start.6 = (f32[16,8,128]{2,1,0:T(8,128)S(1)}, f32[16,8,128]{2,1,0:T(8,128)}, u32[]{:S(2)}) copy-start(f32[16,8,128]{2,1,0:T(8,128)} %param.29) | copy-start | bytes 196612
  37.8 214.2 %copy-start.7 = (f32[16,8,128]{2,1,0:T(8,128)S(1)}, f32[16,8,128]{2,1,0:T(8,128)}, u32[]{:S(2)}) copy-start(f32[16,8,128]{2,1,0:T(8,128)} %param.30) | copy-start | bytes 196612
  37.8 226.8 %copy-start.12 = (f32[7680]{0:T(1024)S(1)}, f32[7680]{0:T(1024)}, u32[]{:S(2)}) copy-start(f32[7680]{0:T(1024)} %param.39) | copy-start | bytes 92164
  252.1 2.6 collective-permute-start.8
  253.4 6.3 collective-permute-start.9
  259.7 5.0 collective-permute-start.10
  263.2 5.6 collective-permute-start.11
  268.8 219.0 %copy-start.8 = (f32[3,7680]{1,0:T(4,128)S(1)}, f32[3,7680]{1,0:T(4,128)}, u32[]{:S(2)}) copy-start(f32[3,7680]{1,0:T(4,128)} %param.40) | copy-start | bytes 276484
  268.8 219.0 %copy-start.9 = (f32[3,7680]{1,0:T(4,128)S(1)}, f32[3,7680]{1,0:T(4,128)}, u32[]{:S(2)}) copy-start(f32[3,7680]{1,0:T(4,128)} %param.38) | copy-start | bytes 276484
  268.8 219.0 %copy-start.10 = (f32[3,7680]{1,0:T(4,128)S(1)}, f32[3,7680]{1,0:T(4,128)}, u32[]{:S(2)}) copy-start(f32[3,7680]{1,0:T(4,128)} %param.37) | copy-start | bytes 276484
  268.9 227.0 %copy-start.5 = (s32[16,8,128]{2,1,0:T(8,128)S(1)}, s32[16,8,128]{2,1,0:T(8,128)}, u32[]{:S(2)}) copy-start(s32[16,8,128]{2,1,0:T(8,128)} %param.36) | copy-start | bytes 196612
  483.7 16.3 %copy-start.2 = (f32[16,8,128]{2,1,0:T(8,128)}, f32[16,8,128]{2,1,0:T(8,128)S(1)}, u32[]{:S(2)}) copy-start(f32[16,8,128]{2,1,0:T(8,128)S(1)} %get-tuple-element.360) | copy-start | bytes 196612
  483.7 5.2 collective-permute-start.12
  486.5 4.3 collective-permute-start.13
  488.8 464.7 %all-reduce.2.cloned.1.call-start = ((), (), s32[]{:S(2)}) async-start(), calls=%async_computation.1 | async-start | bytes 1966080 | tf_op jit(solution)/shard_map/psum | solution.py:123
  490.8 5.1 collective-permute-start.14
  494.3 5.6 collective-permute-start.15
  499.9 214.2 %copy-start.11 = (s32[16,8,128]{2,1,0:T(8,128)S(1)}, s32[16,8,128]{2,1,0:T(8,128)}, u32[]{:S(2)}) copy-start(s32[16,8,128]{2,1,0:T(8,128)} %param.35) | copy-start | bytes 196612
  499.9 214.2 %copy-start = (f32[3,16,8,128]{3,2,1,0:T(8,128)S(1)}, f32[3,16,8,128]{3,2,1,0:T(8,128)}, u32[]{:S(2)}) copy-start(f32[3,16,8,128]{3,2,1,0:T(8,128)} %param.33) | copy-start | bytes 589828
  499.9 214.3 %copy-start.1 = (f32[3,16,8,128]{3,2,1,0:T(8,128)S(1)}, f32[3,16,8,128]{3,2,1,0:T(8,128)}, u32[]{:S(2)}) copy-start(f32[3,16,8,128]{3,2,1,0:T(8,128)} %param.34) | copy-start | bytes 589828
  714.2 5.8 copy-start.3
  814.0 139.5 %copy-start.13 = (f32[3]{0:T(128)S(1)}, f32[3]{0:T(128)}, u32[]{:S(2)}) copy-start(f32[3]{0:T(128)} %constant.120.clone) | copy-start | bytes 40
Sparse Core Ops, SparseCore 0:
  488.9 46.8 all-gather.1
Sparse Core Ops, SparseCore 1:
  823.6 129.8 all-reduce.1
where the time goes:
time: 1130 us
  local copies, waits for them, and re-layouts  359 us (32%)
  other arithmetic  212 us (19%)
  matrix products  193 us (17%)
  loops' own time  163 us (14%)
  waiting for transfers between devices  106 us (9%)
  blocking collectives  41.4 us (4%)
  starting transfers between devices  37.4 us (3%)
  between operations  16.7 us (1%)
    dot_general x48, matrix products, one_row(): jnp.einsum('ckij,ckj->ci', weight, near_val, precision=lax.Precision.HIGH...  193 us
    another operation x3, loops' own time, pair_sums(): return lax.map(one_row, jnp.arange(row_count, dtype=jnp.int32))  163 us
    scatter-add x1, other arithmetic, shards(): jax.ops.segment_sum(stacked, wall_body.reshape(-1), num_segments=BODIES)  94 us
    reduce_sum x48, other arithmetic, one_row(): weight_sum = jnp.sum(weight, axis=(1, 3))  90.2 us
    psum x1, waiting for transfers between devices, shards(): totals, density_error = lax.psum((partials, error_local), ('tile', 'body'))  86.6 us
    gather x1, local copies, waits for them, and re-layouts, shards(): jnp.take(full_state[0:3], index_flat, axis=1).reshape(wall_arm.shape)  59.9 us
    gather x1, local copies, waits for them, and re-layouts, shards(): jnp.take(full_state[3:6], index_flat, axis=1).reshape(wall_arm.shape)  59.8 us
    gather x144, local copies, waits for them, and re-layouts, one_row(): jnp.take_along_axis(jnp.transpose(shifted_pos, (2, 0, 1, 3)), code_list[:...  53 us
  transfers between devices with their start and end apart: 18, of which 7 were waited for; matrix products, arithmetic and copies ran while one was open for 24% of the time, Pallas kernels for 0%

commit v1 on v0

--- a/solution.py
+++ b/solution.py
@@ -120,7 +120,7 @@
     own_params = jnp.concatenate(
         [linear_velocity, angular_velocity, inverse_mass[None], inverse_inertia], 0
     )
-    totals, density_error = lax.psum((partials, error_local), ("tile", "body"))
+    totals, density_error = lax.psum(lax.psum((partials, error_local), "tile"), "body")
     all_params = lax.all_gather(own_params, "body", axis=1, tiled=True)
     full_state = advance(all_params, totals)
     own_state = lax.dynamic_slice_in_dim(full_state, first_owned, owned, 1)

time: 1130 us -> 1110 us (0.982)
  blocking collectives: 41.4 us -> 25.6 us
    psum x1 -> x2, blocking collectives: 41.4 us -> 25.6 us  [the longest x1 12.9 us: shards(): lax.psum(lax.psum((partials, error_local), 'tile'), 'body')]
    psum x1 -> x2, waiting for transfers between devices: 86.6 us -> 77.8 us  [the longest x1 56.1 us: shards(): lax.psum((partials, error_local), 'tile')]
  transfers between devices with their start and end apart: 18 -> 19, of which waited for: 7 -> 8; matrix products, arithmetic and copies ran while one was open for 24% -> 1% of each run, Pallas kernels for 0% -> 0%
where the time goes in v1:
time: 1110 us
  local copies, waits for them, and re-layouts  360 us (32%)
  other arithmetic  212 us (19%)
  matrix products  193 us (17%)
  loops' own time  163 us (15%)
  waiting for transfers between devices  98.4 us (9%)
  starting transfers between devices  37.5 us (3%)
  blocking collectives  25.6 us (2%)
  between operations  16.7 us (2%)
    dot_general x48, matrix products, one_row(): jnp.einsum('ckij,ckj->ci', weight, near_val, precision=lax.Precision.HIGH...  193 us
    another operation x3, loops' own time, pair_sums(): return lax.map(one_row, jnp.arange(row_count, dtype=jnp.int32))  163 us
    scatter-add x1, other arithmetic, shards(): jax.ops.segment_sum(stacked, wall_body.reshape(-1), num_segments=BODIES)  94.1 us
    reduce_sum x48, other arithmetic, one_row(): weight_sum = jnp.sum(weight, axis=(1, 3))  90.2 us
    gather x1, local copies, waits for them, and re-layouts, shards(): jnp.take(full_state[0:3], index_flat, axis=1).reshape(wall_arm.shape)  60.2 us
    gather x1, local copies, waits for them, and re-layouts, shards(): jnp.take(full_state[3:6], index_flat, axis=1).reshape(wall_arm.shape)  60.2 us
    psum x1, waiting for transfers between devices, shards(): lax.psum((partials, error_local), 'tile')  56.1 us
    gather x144, local copies, waits for them, and re-layouts, one_row(): jnp.take_along_axis(jnp.transpose(shifted_pos, (2, 0, 1, 3)), code_list[:...  53 us
  transfers between devices with their start and end apart: 19, of which 8 were waited for; matrix products, arithmetic and copies ran while one was open for 1% of the time, Pallas kernels for 0%

profile of v1, /device:TPU:0, one launch (start us, length us, event | category | flops | bytes accessed | tf_op | source)
XLA Modules:
  0.0 1105.3 jit_solution(7589567651568128614)
XLA Ops:
  13.8 4.5 collective-permute-start
  27.3 4.5 collective-permute-start.2
  33.4 4.2 collective-permute-done.3
  37.8 214.1 %while.36 = (s32[]{:T(128)}, f32[16,8,128]{2,1,0:T(8,128)S(1)}, f32[16,8,128]{2,1,0:T(8,128)S(1)}, s32[16]{0:T(128)S(1)}, f32[3,16,8,128]{3,2,1,0:T(8,128)}, /*i...) while((s32[]{:T(128)}, f32[16,8,128]{2,1,0:T(8,128)S(1)}, ...), condition=%wide.region_2.0_spmd, body=%wide.region_0.4_spmd.sunk | while | flops 27549932 | bytes 1204188 | solution.py:61
  47.2 4.0 fusion.81
  74.0 4.0 fusion.81
  87.4 4.0 fusion.81
  100.7 4.0 fusion.81
  114.1 4.0 fusion.81
  127.5 4.0 fusion.81
  140.9 4.0 fusion.81
  154.3 4.0 fusion.81
  167.7 4.0 fusion.81
  194.4 4.0 fusion.81
  254.7 5.0 collective-permute-done.9
  264.6 4.1 collective-permute-done.11
  268.8 214.1 %while.37 = (s32[]{:T(128)}, f32[16,8,128]{2,1,0:T(8,128)S(1)}, f32[16,8,128]{2,1,0:T(8,128)S(1)}, s32[16]{0:T(128)S(1)}, f32[3,16,8,128]{3,2,1,0:T(8,128)}, /*i...) while((s32[]{:T(128)}, f32[16,8,128]{2,1,0:T(8,128)S(1)}, ...), condition=%wide.region_5.8_spmd, body=%wide.region_3.7_spmd.sunk | while | flops 27549932 | bytes 1204188 | solution.py:61
  278.2 4.0 fusion.85
  291.5 4.0 fusion.85
  304.9 4.0 fusion.85
  318.3 4.0 fusion.85
  331.7 4.0 fusion.85
  345.1 4.0 fusion.85
  358.4 4.0 fusion.85
  371.8 4.0 fusion.85
  385.2 4.0 fusion.85
  398.6 4.0 fusion.85
  412.0 4.0 fusion.85
  425.4 4.0 fusion.85
  438.7 4.0 fusion.85
  452.1 4.0 fusion.85
  465.5 4.0 fusion.85
  478.9 4.0 fusion.85
  499.9 214.1 %while.38 = (s32[]{:T(128)}, f32[16,8,128]{2,1,0:T(8,128)S(1)}, f32[16,8,128]{2,1,0:T(8,128)S(1)}, s32[16]{0:T(128)S(1)}, f32[3,16,8,128]{3,2,1,0:T(8,128)}, /*i...) while((s32[]{:T(128)}, f32[16,8,128]{2,1,0:T(8,128)S(1)}, ...), condition=%wide.region_8.11_spmd, body=%wide.region_6.10_spmd.sunk | while | flops 27549932 | bytes 1204188 | solution.py:61
  714.5 5.3 copy.268
  719.8 94.1 %scatter_custom_fusion = f32[30720,6]{1,0:T(8,128)} fusion(s32[16384]{0:T(1024)S(1)} %bitcast.478, f32[16384,6]{1,0:T(8,128)} %copy.268, f32[]{:T(128)} %constant.113.clone.1), kind=kCustom, calls=%fused_computation.226 | custom fusion | flops 98304 | bytes 737792 | tf_op jit(solution)/shard_map/scatter-add | solution.py:117
  813.9 9.6 copy.269
  824.6 56.1 %all-reduce.3.cloned.1.call-done = f32[6,30720]{1,0:T(8,128)} async-done(((f32[6,30720]{1,0:T(8,128)}), f32[6,30720]{1,0:T(8,128)}) %all-reduce.3.cloned.1.call-update) | async-done | bytes 737296 | tf_op jit(solution)/shard_map/psum | solution.py:123
  881.5 12.7 %psum.30 = f32[]{:T(128)} all-reduce(f32[]{:T(128)S(6)} %div.15), channel_id=1, replica_groups=mesh['tile'=8,'body'=4] {'tile'}, use_global_device_ids=true, to_apply=%region_13.17 | all-reduce | flops 1 | bytes 8 | tf_op jit(solution)/shard_map/psum | solution.py:123
  894.2 12.9 %psum.31 = f32[]{:T(128)} all-reduce(f32[]{:T(128)} %psum.30), channel_id=1, replica_groups=mesh['tile'=8,'body'=4] {'body'}, use_global_device_ids=true, to_apply=%region_14.18 | all-reduce | flops 1 | bytes 8 | tf_op jit(solution)/shard_map/psum | solution.py:123
  908.4 21.7 %all-reduce.5.cloned.1.call-done = f32[6,30720]{1,0:T(8,128)} async-done(((f32[6,30720]{1,0:T(8,128)}), f32[6,30720]{1,0:T(8,128)}) %all-reduce.5.cloned.1.call-update) | async-done | bytes 737296 | tf_op jit(solution)/shard_map/psum | solution.py:123
  933.4 7.8 copy.271
  941.1 7.7 copy.270
  949.7 60.2 %gather_fusion.7 = f32[16384,3]{1,0:T(8,128)} fusion(f32[3,30720]{0,1:T(8,128)} %copy.271, s32[16384]{0:T(1024)S(1)} %fusion.58), kind=kCustom, calls=%fused_computation.7.clone | custom fusion | bytes 458752 | tf_op jit(solution)/shard_map/jit(_take)/gather | solution.py:129
  1009.9 60.2 %gather_fusion.6 = f32[16384,3]{1,0:T(8,128)} fusion(f32[3,30720]{0,1:T(8,128)} %copy.270, s32[16384]{0:T(1024)S(1)} %fusion.58), kind=kCustom, calls=%fused_computation.2.clone | custom fusion | bytes 458752 | tf_op jit(solution)/shard_map/jit(_take)/gather | solution.py:128
  1070.1 10.8 select_bitcast_fusion.3
  1080.8 11.0 slice_reduce_fusion.1
  1091.9 5.2 copy.272
  (1907 shorter events, 423.9 us)
Async XLA Ops:
  8.0 872.7 %all-reduce.3.cloned.1.call-start = ((), (), s32[]{:S(2)}) async-start(), calls=%async_computation.1 | async-start | bytes 1966080 | tf_op jit(solution)/shard_map/psum | solution.py:123
  8.8 12.5 %collective-permute-start.5 = (f32[1,8,128]{2,1,0:T(8,128)S(1)}, f32[1,8,128]{2,1,0:T(8,128)S(1)}, u32[]{:S(2)}, u32[]{:S(2)}) collective-permute-start(f32[1,8,128]{2,1,0:T(8,128)S(1)} %get-tuple-element.378), channel_id=1, source_target_pairs={{4,0},{8,4},{12,8},{16,12},{20,16},{24,20},{28,24},{5,1},{9,5},{13... | collective-permute-start | bytes 12296 | tf_op jit(solution)/shard_map/ppermute | solution.py:24
  10.0 10.4 collective-permute-start.4
  13.8 12.3 %collective-permute-start = (f32[3,1,8,128]{3,0,2,1:T(4,128)S(1)}, f32[3,1,8,128]{3,0,2,1:T(4,128)S(1)}, u32[]{:S(2)}, u32[]{:S(2)}) collective-permute-start(f32[3,1,8,128]{3,0,2,1:T(4,128)S(1)} %copy.294), channel_id=1, source_target_pairs={{0,4},{4,8},{8,12},{12,16},{16,20},{20,24},{24,28},{1,5},{5,9},{9,... | collective-permute-start | bytes 36872 | tf_op jit(solution)/shard_map/ppermute | solution.py:21
  18.3 8.9 collective-permute-start.1
  21.3 11.8 %collective-permute-start.6 = (f32[18,1,128]{2,1,0:T(1,128)S(1)}, f32[18,1,128]{2,1,0:T(1,128)S(1)}, u32[]{:S(2)}, u32[]{:S(2)}) collective-permute-start(f32[18,1,128]{2,1,0:T(1,128)S(1)} %get-tuple-element.372), channel_id=1, source_target_pairs={{0,1},{1,2},{2,3},{4,5},{5,6},{6,7},{8,9},{9,10},{10,11},{12,13},{... | collective-permute-start | bytes 27656 | tf_op jit(solution)/shard_map/ppermute | solution.py:21
  24.8 8.3 collective-permute-start.7
  27.3 6.2 collective-permute-start.2
  31.8 5.9 collective-permute-start.3
  37.8 214.2 %copy-start.4 = (f32[16,8,128]{2,1,0:T(8,128)S(1)}, f32[16,8,128]{2,1,0:T(8,128)}, u32[]{:S(2)}) copy-start(f32[16,8,128]{2,1,0:T(8,128)} %param.28) | copy-start | bytes 196612
  37.8 214.2 %copy-start.6 = (f32[16,8,128]{2,1,0:T(8,128)S(1)}, f32[16,8,128]{2,1,0:T(8,128)}, u32[]{:S(2)}) copy-start(f32[16,8,128]{2,1,0:T(8,128)} %param.29) | copy-start | bytes 196612
  37.8 214.2 %copy-start.7 = (f32[16,8,128]{2,1,0:T(8,128)S(1)}, f32[16,8,128]{2,1,0:T(8,128)}, u32[]{:S(2)}) copy-start(f32[16,8,128]{2,1,0:T(8,128)} %param.30) | copy-start | bytes 196612
  252.1 2.6 collective-permute-start.8
  253.4 6.3 collective-permute-start.9
  259.7 5.0 collective-permute-start.10
  263.2 5.6 collective-permute-start.11
  268.8 226.9 %copy-start.12 = (f32[7680]{0:T(1024)S(1)}, f32[7680]{0:T(1024)}, u32[]{:S(2)}) copy-start(f32[7680]{0:T(1024)} %param.39) | copy-start | bytes 92164
  483.6 16.3 %copy-start.2 = (f32[16,8,128]{2,1,0:T(8,128)}, f32[16,8,128]{2,1,0:T(8,128)S(1)}, u32[]{:S(2)}) copy-start(f32[16,8,128]{2,1,0:T(8,128)S(1)} %get-tuple-element.360) | copy-start | bytes 196612
  483.6 4.1 collective-permute-start.12
  486.4 4.3 collective-permute-start.13
  490.7 5.1 collective-permute-start.14
  494.2 5.6 collective-permute-start.15
  499.8 214.1 %copy-start.11 = (s32[16,8,128]{2,1,0:T(8,128)S(1)}, s32[16,8,128]{2,1,0:T(8,128)}, u32[]{:S(2)}) copy-start(s32[16,8,128]{2,1,0:T(8,128)} %param.35) | copy-start | bytes 196612
  499.8 214.2 %copy-start = (f32[3,16,8,128]{3,2,1,0:T(8,128)S(1)}, f32[3,16,8,128]{3,2,1,0:T(8,128)}, u32[]{:S(2)}) copy-start(f32[3,16,8,128]{3,2,1,0:T(8,128)} %param.33) | copy-start | bytes 589828
  499.8 214.4 %copy-start.1 = (f32[3,16,8,128]{3,2,1,0:T(8,128)S(1)}, f32[3,16,8,128]{3,2,1,0:T(8,128)}, u32[]{:S(2)}) copy-start(f32[3,16,8,128]{3,2,1,0:T(8,128)} %param.34) | copy-start | bytes 589828
  714.0 5.8 copy-start.3
  714.5 5.3 copy-start.5
  813.9 9.7 copy-start.8
  813.9 9.7 copy-start.9
  813.9 9.7 copy-start.10
  823.4 106.6 %copy-start.13 = (f32[3]{0:T(128)S(1)}, f32[3]{0:T(128)}, u32[]{:S(2)}) copy-start(f32[3]{0:T(128)} %constant.120.clone) | copy-start | bytes 40
  823.5 83.6 %all-gather.2.cloned.1.call-start = ((), (), s32[]{:S(2)}) async-start(), calls=%async_computation | async-start | bytes 2457600 | tf_op jit(solution)/shard_map/all_gather | solution.py:124
  824.5 105.5 %all-reduce.5.cloned.1.call-start = ((), (), s32[]{:S(2)}) async-start(), calls=%async_computation.2 | async-start | bytes 1966080 | tf_op jit(solution)/shard_map/psum | solution.py:123
Sparse Core Ops, SparseCore 0:
  823.6 57.1 all-reduce.2
Sparse Core Ops, SparseCore 1:
  825.5 44.0 all-gather.1
  880.8 49.2 all-reduce.4
